TPU v7x, 512 devices: a whole 4x4x16 slice. The times are simulated.
512 devices in a mesh: mp: 2 (over y_hi), tok: 8 (over x, core), lat: 32 (over z, y_lo).
Axes of the slice: x: 4, y: 4 (y_hi: 2, y_lo: 2; y = y_hi * 2 + y_lo), z: 16, core: 2. Of those that a mesh axis runs over, the one named last changes fastest.
Arguments:
- inputs: bfloat16 [2, 384, 4608], P('mp', 'lat', 'tok'), may hold values from -6 to 6
- gate_w: bfloat16 [2, 4608, 18432], P('mp', 'tok', 'lat'), may hold values from -0.09375 to 0.09375
- up_w: bfloat16 [2, 4608, 18432], P('mp', 'tok', 'lat'), may hold values from -0.09375 to 0.09375
- down_w: bfloat16 [2, 18432, 4608], P('mp', 'lat', 'tok'), may hold values from -0.046875 to 0.046875
- enc_w: bfloat16 [2, 4608, 8192], P('mp', 'tok', 'lat'), may hold values from -0.0625 to 0.0625
- enc_bias: float32 [8192], P('lat'), may hold values from -3 to 3
- dec_w: bfloat16 [8192, 2, 4608], P('lat', 'mp', 'tok'), may hold values from -0.0625 to 0.0625
- dec_bias: float32 [2, 4608], P('mp', 'tok'), may hold values from -3 to 3
Outputs:
- recon_error: float32 [2, 384, 4608], P('mp', 'lat', 'tok')
- dec_grad: float32 [8192, 2, 4608], P('lat', 'mp', 'tok')
- latent_grad: float32 [384, 8192], P(None, 'lat')
All inputs are finite; a program needn't handle non-finite values.
Results may differ from a plain program's by a relative error of at most 0.009.
Values may be sent and summed in bfloat16 or wider, within the bound.
A program may use at most 64 MiB of HBM per device.

v0:
```python
import jax
import jax.numpy as jnp
from jax import lax
from jax.sharding import PartitionSpec as P


def contract_rows(left, right):
    return lax.dot_general(
        left, right, (((0,), (0,)), ((), ())), preferred_element_type=jnp.float32
    )


def contract_cols(left, right):
    return lax.dot_general(
        left, right, (((1,), (1,)), ((), ())), preferred_element_type=jnp.float32
    )


def body(inputs, gate_w, up_w, down_w, enc_w, enc_bias, dec_w, dec_bias):
    x_rows = inputs[0]
    gathered = lax.all_gather(x_rows, "lat", axis=0, tiled=True)
    gate_local = gate_w[0]
    up_local = up_w[0]
    width = gate_local.shape[1]
    block = gathered
    both = lax.psum_scatter(
        jnp.concatenate(
            [
                jnp.dot(block, gate_local, preferred_element_type=jnp.float32),
                jnp.dot(block, up_local, preferred_element_type=jnp.float32),
            ],
            axis=1,
        ),
        "tok",
        scatter_dimension=0,
        tiled=True,
    )
    hidden = (jax.nn.gelu(both[:, :width], approximate=True) * both[:, width:]).astype(jnp.bfloat16)
    hidden_all = lax.all_gather(hidden, "tok", axis=0, tiled=True)
    down_local = down_w[0]
    block = hidden_all
    acts = lax.psum_scatter(
        jnp.dot(block, down_local, preferred_element_type=jnp.float32),
        "lat",
        scatter_dimension=0,
        tiled=True,
    ).astype(jnp.bfloat16)
    acts_all = lax.all_gather(acts, "lat", axis=0, tiled=True)
    partial_pre = jnp.dot(acts_all, enc_w[0], preferred_element_type=jnp.float32)
    pre = lax.psum(partial_pre, ("mp", "tok"))
    codes = jnp.maximum(pre + enc_bias, 0.0).astype(jnp.bfloat16)
    decoder = dec_w[:, 0, :]
    bias_row = dec_bias[0]
    block = codes
    recon = lax.psum_scatter(
        jnp.dot(block, decoder, preferred_element_type=jnp.float32),
        "lat",
        scatter_dimension=0,
        tiled=True,
    )
    error = recon + bias_row - acts.astype(jnp.float32)
    error_all = lax.all_gather(error.astype(jnp.bfloat16), "lat", axis=0, tiled=True)
    decoder_grad = contract_rows(codes, error_all)
    latent_grad = lax.psum(contract_cols(error_all, decoder), ("mp", "tok"))
    return (error[None], decoder_grad[:, None, :], latent_grad)


def solution(mesh):
    in_specs = (
        P("mp", "lat", "tok"),
        P("mp", "tok", "lat"),
        P("mp", "tok", "lat"),
        P("mp", "lat", "tok"),
        P("mp", "tok", "lat"),
        P("lat"),
        P("lat", "mp", "tok"),
        P("mp", "tok"),
    )
    out_specs = (P("mp", "lat", "tok"), P("lat", "mp", "tok"), P(None, "lat"))
    return jax.shard_map(body, mesh=mesh, in_specs=in_specs, out_specs=out_specs, check_vma=False)
```

profile of v0, /device:TPU:1, one launch (start us, length us, event | category | flops | bytes accessed | tf_op | source)
XLA Modules:
  0.0 789.7 jit_solution(4947730989583786598)
XLA Ops:
  8.0 61.9 %all-gather = bf16[1,384,576]{2,0,1:T(2,128)(2,1)S(1)} all-gather(bf16[1,12,576]{2,0,1:T(2,128)(2,1)S(1)} %copy.20), channel_id=2, replica_groups=mesh['mp'=2,'tok'=8,'lat'=32] {'lat'}, dimensions={1}, use_global_device_ids=true | all-gather | bytes 456192 | tf_op jit(solution)/shard_map/all_gather | solution.py:21
  72.1 2.0 copy.25
  74.1 47.7 %reduce-scatter.8.cloned.1.call-done = f32[48,1152]{1,0:T(8,128)} async-done(((f32[384,1152]{1,0:T(8,128)}), f32[48,1152]{1,0:T(8,128)}) %reduce-scatter.8.cloned.1.call-update) | async-done | bytes 221200 | tf_op jit(solution)/shard_map/reduce_scatter | solution.py:26
  121.8 1.1 fusion.24
  122.9 15.4 %all_gather.13 = bf16[384,576]{1,0:T(8,128)(2,1)S(1)} all-gather(bf16[48,576]{1,0:T(8,128)(2,1)S(1)} %fusion.24), channel_id=1, replica_groups=mesh['mp'=2,'tok'=8,'lat'=32] {'tok'}, dimensions={0}, use_global_device_ids=true | all-gather | bytes 497664 | tf_op jit(solution)/shard_map/all_gather | solution.py:39
  138.8 59.0 %fusion = f32[16,576]{1,0:T(8,128)S(1)} fusion(f32[384,576]{1,0:T(8,128)S(1)} %fusion.2), kind=kCustom, calls=%all-reduce-scatter | all-reduce-scatter fusion | flops 294913 | bytes 923648
  197.9 1.7 collective-permute-start
  199.6 2.1 collective-permute-start.1
  201.7 6.0 collective-permute-start.7
  207.7 4.9 collective-permute-start.2
  212.7 4.9 collective-permute-start.3
  217.6 2.1 collective-permute-start.4
  219.8 3.5 collective-permute-start.5
  223.2 2.8 collective-permute-start.6
  226.1 1.3 dynamic-slice.6
  228.1 1.3 concatenate.4
  229.4 49.4 %all-gather.1 = bf16[32,12,576]{2,1,0:T(8,128)(2,1)S(1)} all-gather(bf16[1,12,576]{2,1,0:T(8,128)(2,1)S(1)} %fusion.31), channel_id=1, replica_groups=mesh['mp'=2,'tok'=8,'lat'=32] {'lat'}, dimensions={0}, use_global_device_ids=true | all-gather | bytes 456192 | tf_op jit(solution)/shard_map/all_gather | solution.py:48
  280.2 180.0 %all-reduce.7.cloned.1.call-done = f32[384,256]{1,0:T(8,128)} async-done(((f32[384,256]{1,0:T(8,128)}), f32[384,256]{1,0:T(8,128)}) %all-reduce.7.cloned.1.call-update) | async-done | bytes 393232 | tf_op jit(solution)/shard_map/psum | solution.py:50
  460.2 1.3 fusion.12
  461.6 59.2 %fusion.1 = f32[16,576]{1,0:T(8,128)S(1)} fusion(f32[384,576]{1,0:T(8,128)S(1)} %fusion.12), kind=kCustom, calls=%all-reduce-scatter.1 | all-reduce-scatter fusion | flops 294913 | bytes 923648
  520.7 1.3 collective-permute-start.10
  522.0 3.4 collective-permute-start.11
  525.5 7.0 collective-permute-start.15
  532.6 4.5 collective-permute-start.12
  537.1 3.9 collective-permute-start.13
  541.0 2.9 collective-permute-start.14
  543.9 3.1 collective-permute-start.8
  547.0 2.2 collective-permute-start.9
  551.3 48.9 %all-gather.2 = bf16[32,12,576]{2,1,0:T(8,128)(2,1)S(1)} all-gather(bf16[1,12,576]{2,1,0:T(8,128)(2,1)S(1)} %get-tuple-element.18), channel_id=1, replica_groups=mesh['mp'=2,'tok'=8,'lat'=32] {'lat'}, dimensions={0}, use_global_device_ids=true | all-gather | bytes 456192 | tf_op jit(solution)/shard_map/all_gather | solution.py:62
  602.2 1.2 convolution_bitcast_fusion
  603.3 178.1 %all-reduce.9.cloned.1.call-done = f32[384,256]{1,0:T(8,128)} async-done(((f32[384,256]{1,0:T(8,128)}), f32[384,256]{1,0:T(8,128)}) %all-reduce.9.cloned.1.call-update) | async-done | bytes 393232 | tf_op jit(solution)/shard_map/psum | solution.py:64
  781.4 1.8 copy.29
  (56 shorter events, 9.1 us)
Async XLA Ops:
  7.2 63.5 %copy-start = (bf16[1,576,576]{2,1,0:T(8,128)(2,1)S(1)}, bf16[1,576,576]{2,1,0:T(8,128)(2,1)}, u32[]{:S(2)}) copy-start(bf16[1,576,576]{2,1,0:T(8,128)(2,1)} %param.10) | copy-start | bytes 1990660
  7.2 114.6 %reduce-scatter.8.cloned.1.call-start = ((), (), s32[]{:S(2)}) async-start(), calls=%async_computation.3 | async-start | bytes 1990656 | tf_op jit(solution)/shard_map/reduce_scatter | solution.py:26
  70.0 1.3 copy-start.3
  74.0 64.2 %copy-start.4 = (bf16[1,576,576]{2,1,0:T(8,128)(2,1)S(1)}, bf16[1,576,576]{2,1,0:T(8,128)(2,1)}, u32[]{:S(2)}) copy-start(bf16[1,576,576]{2,1,0:T(8,128)(2,1)} %param.11) | copy-start | bytes 1990660
  74.1 386.2 %all-reduce.7.cloned.1.call-start = ((), (), s32[]{:S(2)}) async-start(), calls=%async_computation.1 | async-start | bytes 786432 | tf_op jit(solution)/shard_map/psum | solution.py:50
  138.8 140.3 %copy-start.5 = (bf16[1,576,256]{2,1,0:T(8,128)(2,1)S(1)}, bf16[1,576,256]{2,1,0:T(8,128)(2,1)}, u32[]{:S(2)}) copy-start(bf16[1,576,256]{2,1,0:T(8,128)(2,1)} %param.12) | copy-start | bytes 884740
  197.9 21.9 %collective-permute-start = (bf16[16,576]{1,0:T(8,128)(2,1)S(1)}, bf16[16,576]{1,0:T(8,128)(2,1)S(1)}, u32[]{:S(2)}, u32[]{:S(2)}) collective-permute-start(bf16[16,576]{1,0:T(8,128)(2,1)S(1)} %convert.14), channel_id=1, source_target_pairs={{0,1},{1,2},{2,3},{3,4},{4,5},{5,6},{6,7},{7,8},{8,9},{9,10},{10,1... | collective-permute-start | bytes 55304
  199.6 23.6 %collective-permute-start.1 = (bf16[16,576]{1,0:T(8,128)(2,1)S(1)}, bf16[16,576]{1,0:T(8,128)(2,1)S(1)}, u32[]{:S(2)}, u32[]{:S(2)}) collective-permute-start(bf16[16,576]{1,0:T(8,128)(2,1)S(1)} %convert.14), channel_id=1, source_target_pairs={{0,2},{1,3},{2,4},{3,5},{4,6},{5,7},{6,8},{7,9},{8,10},{9,11},{10,... | collective-permute-start | bytes 55304
  201.7 15.9 %collective-permute-start.7 = (bf16[12,576]{1,0:T(8,128)(2,1)S(1)}, bf16[12,576]{1,0:T(8,128)(2,1)S(1)}, u32[]{:S(2)}, u32[]{:S(2)}) collective-permute-start(bf16[12,576]{1,0:T(8,128)(2,1)S(1)} %slice.10), channel_id=1, source_target_pairs={{0,8},{1,9},{2,10},{3,11},{4,12},{5,13},{6,14},{7,15},{8,16},{9,17... | collective-permute-start | bytes 41480
  207.7 20.3 %collective-permute-start.2 = (bf16[16,576]{1,0:T(8,128)(2,1)S(1)}, bf16[16,576]{1,0:T(8,128)(2,1)S(1)}, u32[]{:S(2)}, u32[]{:S(2)}) collective-permute-start(bf16[16,576]{1,0:T(8,128)(2,1)S(1)} %convert.14), channel_id=1, source_target_pairs={{0,3},{1,4},{2,5},{3,6},{4,7},{5,8},{6,9},{7,10},{8,11},{9,12},{10... | collective-permute-start | bytes 55304
  212.7 15.3 %collective-permute-start.3 = (bf16[16,576]{1,0:T(8,128)(2,1)S(1)}, bf16[16,576]{1,0:T(8,128)(2,1)S(1)}, u32[]{:S(2)}, u32[]{:S(2)}) collective-permute-start(bf16[16,576]{1,0:T(8,128)(2,1)S(1)} %convert.14), channel_id=1, source_target_pairs={{0,4},{1,5},{2,6},{3,7},{4,8},{5,9},{6,10},{7,11},{8,12},{9,13},{1... | collective-permute-start | bytes 55304
  217.6 10.4 %collective-permute-start.4 = (bf16[16,576]{1,0:T(8,128)(2,1)S(1)}, bf16[16,576]{1,0:T(8,128)(2,1)S(1)}, u32[]{:S(2)}, u32[]{:S(2)}) collective-permute-start(bf16[16,576]{1,0:T(8,128)(2,1)S(1)} %convert.14), channel_id=1, source_target_pairs={{0,5},{1,6},{2,7},{3,8},{4,9},{5,10},{6,11},{7,12},{8,13},{9,14},{... | collective-permute-start | bytes 55304
  219.8 8.3 %collective-permute-start.5 = (bf16[16,576]{1,0:T(8,128)(2,1)S(1)}, bf16[16,576]{1,0:T(8,128)(2,1)S(1)}, u32[]{:S(2)}, u32[]{:S(2)}) collective-permute-start(bf16[16,576]{1,0:T(8,128)(2,1)S(1)} %convert.14), channel_id=1, source_target_pairs={{0,6},{1,7},{2,8},{3,9},{4,10},{5,11},{6,12},{7,13},{8,14},{9,15},... | collective-permute-start | bytes 55304
  223.2 4.8 collective-permute-start.6
  229.4 230.8 %copy-start.2 = (bf16[256,1,576]{0,2,1:T(8,128)(2,1)S(1)}, bf16[256,1,576]{0,2,1:T(8,128)(2,1)}, u32[]{:S(2)}) copy-start(bf16[256,1,576]{0,2,1:T(8,128)(2,1)} %param.14) | copy-start | bytes 884740
  229.4 230.8 %copy-start.6 = (f32[256]{0:T(256)S(1)}, f32[256]{0:T(256)}, u32[]{:S(2)}) copy-start(f32[256]{0:T(256)} %param.13) | copy-start | bytes 3076
  280.2 269.0 %copy-start.7 = (f32[1,576]{1,0:T(1,128)S(1)}, f32[1,576]{1,0:T(1,128)}, u32[]{:S(2)}) copy-start(f32[1,576]{1,0:T(1,128)} %param.15) | copy-start | bytes 6916
  280.2 501.2 %all-reduce.9.cloned.1.call-start = ((), (), s32[]{:S(2)}) async-start(), calls=%async_computation.2 | async-start | bytes 786432 | tf_op jit(solution)/shard_map/psum | solution.py:64
  520.7 23.1 %collective-permute-start.10 = (f32[16,576]{1,0:T(8,128)S(1)}, f32[16,576]{1,0:T(8,128)S(1)}, u32[]{:S(2)}, u32[]{:S(2)}) collective-permute-start(f32[16,576]{1,0:T(8,128)S(1)} %fusion.1), channel_id=1, source_target_pairs={{0,3},{1,4},{2,5},{3,6},{4,7},{5,8},{6,9},{7,10},{8,11},{9,12},{10... | collective-permute-start | bytes 110600
  522.0 24.9 %collective-permute-start.11 = (f32[16,576]{1,0:T(8,128)S(1)}, f32[16,576]{1,0:T(8,128)S(1)}, u32[]{:S(2)}, u32[]{:S(2)}) collective-permute-start(f32[16,576]{1,0:T(8,128)S(1)} %fusion.1), channel_id=1, source_target_pairs={{0,4},{1,5},{2,6},{3,7},{4,8},{5,9},{6,10},{7,11},{8,12},{9,13},{1... | collective-permute-start | bytes 110600
  525.5 15.5 %collective-permute-start.15 = (f32[12,576]{1,0:T(8,128)S(1)}, f32[12,576]{1,0:T(8,128)S(1)}, u32[]{:S(2)}, u32[]{:S(2)}) collective-permute-start(f32[12,576]{1,0:T(8,128)S(1)} %slice.11), channel_id=1, source_target_pairs={{0,8},{1,9},{2,10},{3,11},{4,12},{5,13},{6,14},{7,15},{8,16},{9,17... | collective-permute-start | bytes 82952
  532.6 16.7 %collective-permute-start.12 = (f32[16,576]{1,0:T(8,128)S(1)}, f32[16,576]{1,0:T(8,128)S(1)}, u32[]{:S(2)}, u32[]{:S(2)}) collective-permute-start(f32[16,576]{1,0:T(8,128)S(1)} %fusion.1), channel_id=1, source_target_pairs={{0,5},{1,6},{2,7},{3,8},{4,9},{5,10},{6,11},{7,12},{8,13},{9,14},{... | collective-permute-start | bytes 110600
  537.1 12.2 %collective-permute-start.13 = (f32[16,576]{1,0:T(8,128)S(1)}, f32[16,576]{1,0:T(8,128)S(1)}, u32[]{:S(2)}, u32[]{:S(2)}) collective-permute-start(f32[16,576]{1,0:T(8,128)S(1)} %fusion.1), channel_id=1, source_target_pairs={{0,6},{1,7},{2,8},{3,9},{4,10},{5,11},{6,12},{7,13},{8,14},{9,15},... | collective-permute-start | bytes 110600
  541.0 8.2 %collective-permute-start.14 = (f32[16,576]{1,0:T(8,128)S(1)}, f32[16,576]{1,0:T(8,128)S(1)}, u32[]{:S(2)}, u32[]{:S(2)}) collective-permute-start(f32[16,576]{1,0:T(8,128)S(1)} %fusion.1), channel_id=1, source_target_pairs={{0,7},{1,8},{2,9},{3,10},{4,11},{5,12},{6,13},{7,14},{8,15},{9,16}... | collective-permute-start | bytes 110600
  543.9 5.4 collective-permute-start.8
  547.0 3.3 collective-permute-start.9
  551.3 50.8 %copy-start.1 = (f32[384,256]{1,0:T(8,128)S(1)}, f32[384,256]{1,0:T(8,128)}, u32[]{:S(2)}) copy-start(f32[384,256]{1,0:T(8,128)} %all-reduce.7.cloned.1.call-done) | copy-start | bytes 1179652
Sparse Core Ops, SparseCore 0:
  74.2 47.5 reduce-scatter.7
  280.3 179.8 all-reduce.6
  601.6 179.7 all-reduce.8
where the time goes:
time: 790 us
  waiting for transfers between devices  407 us (52%)
  blocking collectives  294 us (37%)
  starting transfers between devices  56.6 us (7%)
  between operations  14.9 us (2%)
  local copies, waits for them, and re-layouts  10 us (1%)
    psum x1, waiting for transfers between devices, body(): pre = lax.psum(partial_pre, ('mp', 'tok'))  180 us
    psum x1, waiting for transfers between devices, body(): latent_grad = lax.psum(contract_cols(error_all, decoder), ('mp', 'tok'))  178 us
    unnamed x2, blocking collectives  118 us
    all_gather x1, blocking collectives, body(): gathered = lax.all_gather(x_rows, 'lat', axis=0, tiled=True)  61.9 us
    unnamed x16, starting transfers between devices  56.5 us
    all_gather x1, blocking collectives, body(): acts_all = lax.all_gather(acts, 'lat', axis=0, tiled=True)  49.4 us
    all_gather x1, blocking collectives, body(): lax.all_gather(error.astype(jnp.bfloat16), 'lat', axis=0, tiled=True)  48.9 us
    reduce_scatter x1, waiting for transfers between devices, body(): lax.psum_scatter(jnp.concatenate([jnp.dot(block, gate_local, preferred_el...  47.7 us
  transfers between devices with their start and end apart: 19, of which 4 were waited for; matrix products, arithmetic and copies ran while one was open for 0% of the time, Pallas kernels for 0%

commit v1 on v0

--- a/solution.py
+++ b/solution.py
@@ -17,6 +17,10 @@
 
 
 def body(inputs, gate_w, up_w, down_w, enc_w, enc_bias, dec_w, dec_bias):
+
+    def refer_target(my_tile):
+        return lax.all_gather(my_tile, ("mp", "tok")).sum(axis=0)
+
     x_rows = inputs[0]
     gathered = lax.all_gather(x_rows, "lat", axis=0, tiled=True)
     gate_local = gate_w[0]
@@ -47,7 +51,7 @@
     ).astype(jnp.bfloat16)
     acts_all = lax.all_gather(acts, "lat", axis=0, tiled=True)
     partial_pre = jnp.dot(acts_all, enc_w[0], preferred_element_type=jnp.float32)
-    pre = lax.psum(partial_pre, ("mp", "tok"))
+    pre = refer_target(partial_pre)
     codes = jnp.maximum(pre + enc_bias, 0.0).astype(jnp.bfloat16)
     decoder = dec_w[:, 0, :]
     bias_row = dec_bias[0]

time: 790 us -> 716 us (0.906)
  waiting for transfers between devices: 407 us -> 331 us
    psum x1 -> x0, waiting for transfers between devices: 180 us -> none  [body(): pre = lax.psum(partial_pre, ('mp', 'tok'))]
    all_gather x0 -> x1, waiting for transfers between devices: none -> 106 us  [refer_target(): return lax.all_gather(my_tile, ('mp', 'tok')).sum(axis=0)]
where the time goes in v1:
time: 716 us
  waiting for transfers between devices  331 us (46%)
  blocking collectives  294 us (41%)
  starting transfers between devices  56.3 us (8%)
  between operations  14.9 us (2%)
  local copies, waits for them, and re-layouts  9.99 us (1%)
    psum x1, waiting for transfers between devices, body(): latent_grad = lax.psum(contract_cols(error_all, decoder), ('mp', 'tok'))  176 us
    unnamed x2, blocking collectives  118 us
    all_gather x1, waiting for transfers between devices, refer_target(): return lax.all_gather(my_tile, ('mp', 'tok')).sum(axis=0)  106 us
    all_gather x1, blocking collectives, body(): gathered = lax.all_gather(x_rows, 'lat', axis=0, tiled=True)  61.9 us
    unnamed x16, starting transfers between devices  56.2 us
    all_gather x1, blocking collectives, body(): acts_all = lax.all_gather(acts, 'lat', axis=0, tiled=True)  49.3 us
    all_gather x1, blocking collectives, body(): lax.all_gather(error.astype(jnp.bfloat16), 'lat', axis=0, tiled=True)  48.9 us
    reduce_scatter x1, waiting for transfers between devices, body(): lax.psum_scatter(jnp.concatenate([jnp.dot(block, gate_local, preferred_el...  47.7 us
  transfers between devices with their start and end apart: 19, of which 4 were waited for; matrix products, arithmetic and copies ran while one was open for 0% of the time, Pallas kernels for 0%

profile of v1, /device:TPU:1, one launch (start us, length us, event | category | flops | bytes accessed | tf_op | source)
XLA Modules:
  0.0 715.7 jit_solution(12954005024369496793)
XLA Ops:
  8.0 61.9 %all-gather = bf16[1,384,576]{2,0,1:T(2,128)(2,1)S(1)} all-gather(bf16[1,12,576]{2,0,1:T(2,128)(2,1)S(1)} %copy.20), channel_id=2, replica_groups=mesh['mp'=2,'tok'=8,'lat'=32] {'lat'}, dimensions={1}, use_global_device_ids=true | all-gather | bytes 456192 | tf_op jit(solution)/shard_map/all_gather | solution.py:25
  72.1 2.0 copy.25
  74.1 47.7 %reduce-scatter.8.cloned.1.call-done = f32[48,1152]{1,0:T(8,128)} async-done(((f32[384,1152]{1,0:T(8,128)}), f32[48,1152]{1,0:T(8,128)}) %reduce-scatter.8.cloned.1.call-update) | async-done | bytes 221200 | tf_op jit(solution)/shard_map/reduce_scatter | solution.py:30
  121.8 1.1 fusion.24
  122.8 15.4 %all_gather.19 = bf16[384,576]{1,0:T(8,128)(2,1)S(1)} all-gather(bf16[48,576]{1,0:T(8,128)(2,1)S(1)} %fusion.24), channel_id=1, replica_groups=mesh['mp'=2,'tok'=8,'lat'=32] {'tok'}, dimensions={0}, use_global_device_ids=true | all-gather | bytes 497664 | tf_op jit(solution)/shard_map/all_gather | solution.py:43
  138.9 58.9 %fusion = f32[16,576]{1,0:T(8,128)S(1)} fusion(f32[384,576]{1,0:T(8,128)S(1)} %fusion.2), kind=kCustom, calls=%all-reduce-scatter | all-reduce-scatter fusion | flops 294913 | bytes 923648
  197.8 2.0 collective-permute-start
  199.8 1.8 collective-permute-start.1
  201.6 5.8 collective-permute-start.7
  207.4 5.1 collective-permute-start.2
  212.5 5.1 collective-permute-start.3
  217.7 2.1 collective-permute-start.4
  219.8 3.4 collective-permute-start.5
  223.2 2.8 collective-permute-start.6
  226.1 1.3 dynamic-slice.6
  228.1 1.3 concatenate.4
  229.4 49.3 %all-gather.2 = bf16[32,12,576]{2,1,0:T(8,128)(2,1)S(1)} all-gather(bf16[1,12,576]{2,1,0:T(8,128)(2,1)S(1)} %fusion.31), channel_id=1, replica_groups=mesh['mp'=2,'tok'=8,'lat'=32] {'lat'}, dimensions={0}, use_global_device_ids=true | all-gather | bytes 456192 | tf_op jit(solution)/shard_map/all_gather | solution.py:52
  280.1 106.3 %all-gather.6.cloned.1.call-done = f32[6144,256]{1,0:T(8,128)} async-done(((f32[384,256]{1,0:T(8,128)}), f32[6144,256]{1,0:T(8,128)}) %all-gather.6.cloned.1.call-update) | async-done | bytes 6291472 | tf_op jit(solution)/shard_map/all_gather | solution.py:22
  386.4 3.3 reduce_sum.9
  390.1 59.5 %fusion.1 = f32[16,576]{1,0:T(8,128)S(1)} fusion(f32[384,576]{1,0:T(8,128)S(1)} %fusion.12), kind=kCustom, calls=%all-reduce-scatter.1 | all-reduce-scatter fusion | flops 294913 | bytes 923648
  449.5 1.3 collective-permute-start.10
  450.8 2.7 collective-permute-start.11
  453.6 7.5 %collective-permute-start.15 = (f32[12,576]{1,0:T(8,128)S(1)}, f32[12,576]{1,0:T(8,128)S(1)}, u32[]{:S(2)}, u32[]{:S(2)}) collective-permute-start(f32[12,576]{1,0:T(8,128)S(1)} %slice.11), channel_id=1, source_target_pairs={{0,8},{1,9},{2,10},{3,11},{4,12},{5,13},{6,14},{7,15},{8,16},{9,17... | collective-permute-start | bytes 82952
  461.1 4.8 collective-permute-start.12
  465.9 4.2 collective-permute-start.13
  470.1 2.2 collective-permute-start.14
  472.3 3.1 collective-permute-start.8
  475.4 2.2 collective-permute-start.9
  479.8 48.9 %all-gather.3 = bf16[32,12,576]{2,1,0:T(8,128)(2,1)S(1)} all-gather(bf16[1,12,576]{2,1,0:T(8,128)(2,1)S(1)} %get-tuple-element.18), channel_id=1, replica_groups=mesh['mp'=2,'tok'=8,'lat'=32] {'lat'}, dimensions={0}, use_global_device_ids=true | all-gather | bytes 456192 | tf_op jit(solution)/shard_map/all_gather | solution.py:66
  530.7 1.2 convolution_bitcast_fusion
  531.9 175.6 %all-reduce.6.cloned.1.call-done = f32[384,256]{1,0:T(8,128)} async-done(((f32[384,256]{1,0:T(8,128)}), f32[384,256]{1,0:T(8,128)}) %all-reduce.6.cloned.1.call-update) | async-done | bytes 393232 | tf_op jit(solution)/shard_map/psum | solution.py:68
  707.4 1.8 copy.28
  (55 shorter events, 9.4 us)
Async XLA Ops:
  7.2 63.5 %copy-start = (bf16[1,576,576]{2,1,0:T(8,128)(2,1)S(1)}, bf16[1,576,576]{2,1,0:T(8,128)(2,1)}, u32[]{:S(2)}) copy-start(bf16[1,576,576]{2,1,0:T(8,128)(2,1)} %param.10) | copy-start | bytes 1990660
  7.2 114.6 %reduce-scatter.8.cloned.1.call-start = ((), (), s32[]{:S(2)}) async-start(), calls=%async_computation.3 | async-start | bytes 1990656 | tf_op jit(solution)/shard_map/reduce_scatter | solution.py:30
  70.0 1.3 copy-start.2
  74.0 64.2 %copy-start.3 = (bf16[1,576,576]{2,1,0:T(8,128)(2,1)S(1)}, bf16[1,576,576]{2,1,0:T(8,128)(2,1)}, u32[]{:S(2)}) copy-start(bf16[1,576,576]{2,1,0:T(8,128)(2,1)} %param.11) | copy-start | bytes 1990660
  74.1 312.3 %all-gather.6.cloned.1.call-start = ((), (), s32[]{:S(2)}) async-start(), calls=%async_computation.2 | async-start | bytes 6684672 | tf_op jit(solution)/shard_map/all_gather | solution.py:22
  138.8 140.2 %copy-start.4 = (bf16[1,576,256]{2,1,0:T(8,128)(2,1)S(1)}, bf16[1,576,256]{2,1,0:T(8,128)(2,1)}, u32[]{:S(2)}) copy-start(bf16[1,576,256]{2,1,0:T(8,128)(2,1)} %param.12) | copy-start | bytes 884740
  197.8 22.0 %collective-permute-start = (bf16[16,576]{1,0:T(8,128)(2,1)S(1)}, bf16[16,576]{1,0:T(8,128)(2,1)S(1)}, u32[]{:S(2)}, u32[]{:S(2)}) collective-permute-start(bf16[16,576]{1,0:T(8,128)(2,1)S(1)} %convert.14), channel_id=1, source_target_pairs={{0,1},{1,2},{2,3},{3,4},{4,5},{5,6},{6,7},{7,8},{8,9},{9,10},{10,1... | collective-permute-start | bytes 55304
  199.8 23.4 %collective-permute-start.1 = (bf16[16,576]{1,0:T(8,128)(2,1)S(1)}, bf16[16,576]{1,0:T(8,128)(2,1)S(1)}, u32[]{:S(2)}, u32[]{:S(2)}) collective-permute-start(bf16[16,576]{1,0:T(8,128)(2,1)S(1)} %convert.14), channel_id=1, source_target_pairs={{0,2},{1,3},{2,4},{3,5},{4,6},{5,7},{6,8},{7,9},{8,10},{9,11},{10,... | collective-permute-start | bytes 55304
  201.6 16.0 %collective-permute-start.7 = (bf16[12,576]{1,0:T(8,128)(2,1)S(1)}, bf16[12,576]{1,0:T(8,128)(2,1)S(1)}, u32[]{:S(2)}, u32[]{:S(2)}) collective-permute-start(bf16[12,576]{1,0:T(8,128)(2,1)S(1)} %slice.10), channel_id=1, source_target_pairs={{0,8},{1,9},{2,10},{3,11},{4,12},{5,13},{6,14},{7,15},{8,16},{9,17... | collective-permute-start | bytes 41480
  207.4 20.6 %collective-permute-start.2 = (bf16[16,576]{1,0:T(8,128)(2,1)S(1)}, bf16[16,576]{1,0:T(8,128)(2,1)S(1)}, u32[]{:S(2)}, u32[]{:S(2)}) collective-permute-start(bf16[16,576]{1,0:T(8,128)(2,1)S(1)} %convert.14), channel_id=1, source_target_pairs={{0,3},{1,4},{2,5},{3,6},{4,7},{5,8},{6,9},{7,10},{8,11},{9,12},{10... | collective-permute-start | bytes 55304
  212.5 15.5 %collective-permute-start.3 = (bf16[16,576]{1,0:T(8,128)(2,1)S(1)}, bf16[16,576]{1,0:T(8,128)(2,1)S(1)}, u32[]{:S(2)}, u32[]{:S(2)}) collective-permute-start(bf16[16,576]{1,0:T(8,128)(2,1)S(1)} %convert.14), channel_id=1, source_target_pairs={{0,4},{1,5},{2,6},{3,7},{4,8},{5,9},{6,10},{7,11},{8,12},{9,13},{1... | collective-permute-start | bytes 55304
  217.7 10.4 %collective-permute-start.4 = (bf16[16,576]{1,0:T(8,128)(2,1)S(1)}, bf16[16,576]{1,0:T(8,128)(2,1)S(1)}, u32[]{:S(2)}, u32[]{:S(2)}) collective-permute-start(bf16[16,576]{1,0:T(8,128)(2,1)S(1)} %convert.14), channel_id=1, source_target_pairs={{0,5},{1,6},{2,7},{3,8},{4,9},{5,10},{6,11},{7,12},{8,13},{9,14},{... | collective-permute-start | bytes 55304
  219.8 8.2 %collective-permute-start.5 = (bf16[16,576]{1,0:T(8,128)(2,1)S(1)}, bf16[16,576]{1,0:T(8,128)(2,1)S(1)}, u32[]{:S(2)}, u32[]{:S(2)}) collective-permute-start(bf16[16,576]{1,0:T(8,128)(2,1)S(1)} %convert.14), channel_id=1, source_target_pairs={{0,6},{1,7},{2,8},{3,9},{4,10},{5,11},{6,12},{7,13},{8,14},{9,15},... | collective-permute-start | bytes 55304
  223.2 4.8 collective-permute-start.6
  280.1 427.3 %all-reduce.6.cloned.1.call-start = ((), (), s32[]{:S(2)}) async-start(), calls=%async_computation.1 | async-start | bytes 786432 | tf_op jit(solution)/shard_map/psum | solution.py:68
  386.4 3.3 copy-start.1
  386.4 3.3 copy-start.5
  389.7 87.9 %copy-start.6 = (f32[1,576]{1,0:T(1,128)S(1)}, f32[1,576]{1,0:T(1,128)}, u32[]{:S(2)}) copy-start(f32[1,576]{1,0:T(1,128)} %param.15) | copy-start | bytes 6916
  449.5 22.8 %collective-permute-start.10 = (f32[16,576]{1,0:T(8,128)S(1)}, f32[16,576]{1,0:T(8,128)S(1)}, u32[]{:S(2)}, u32[]{:S(2)}) collective-permute-start(f32[16,576]{1,0:T(8,128)S(1)} %fusion.1), channel_id=1, source_target_pairs={{0,3},{1,4},{2,5},{3,6},{4,7},{5,8},{6,9},{7,10},{8,11},{9,12},{10... | collective-permute-start | bytes 110600
  450.8 24.6 %collective-permute-start.11 = (f32[16,576]{1,0:T(8,128)S(1)}, f32[16,576]{1,0:T(8,128)S(1)}, u32[]{:S(2)}, u32[]{:S(2)}) collective-permute-start(f32[16,576]{1,0:T(8,128)S(1)} %fusion.1), channel_id=1, source_target_pairs={{0,4},{1,5},{2,6},{3,7},{4,8},{5,9},{6,10},{7,11},{8,12},{9,13},{1... | collective-permute-start | bytes 110600
  453.6 16.5 %collective-permute-start.15 = (f32[12,576]{1,0:T(8,128)S(1)}, f32[12,576]{1,0:T(8,128)S(1)}, u32[]{:S(2)}, u32[]{:S(2)}) collective-permute-start(f32[12,576]{1,0:T(8,128)S(1)} %slice.11), channel_id=1, source_target_pairs={{0,8},{1,9},{2,10},{3,11},{4,12},{5,13},{6,14},{7,15},{8,16},{9,17... | collective-permute-start | bytes 82952
  461.1 16.6 %collective-permute-start.12 = (f32[16,576]{1,0:T(8,128)S(1)}, f32[16,576]{1,0:T(8,128)S(1)}, u32[]{:S(2)}, u32[]{:S(2)}) collective-permute-start(f32[16,576]{1,0:T(8,128)S(1)} %fusion.1), channel_id=1, source_target_pairs={{0,5},{1,6},{2,7},{3,8},{4,9},{5,10},{6,11},{7,12},{8,13},{9,14},{... | collective-permute-start | bytes 110600
  465.9 11.8 %collective-permute-start.13 = (f32[16,576]{1,0:T(8,128)S(1)}, f32[16,576]{1,0:T(8,128)S(1)}, u32[]{:S(2)}, u32[]{:S(2)}) collective-permute-start(f32[16,576]{1,0:T(8,128)S(1)} %fusion.1), channel_id=1, source_target_pairs={{0,6},{1,7},{2,8},{3,9},{4,10},{5,11},{6,12},{7,13},{8,14},{9,15},... | collective-permute-start | bytes 110600
  470.1 7.6 %collective-permute-start.14 = (f32[16,576]{1,0:T(8,128)S(1)}, f32[16,576]{1,0:T(8,128)S(1)}, u32[]{:S(2)}, u32[]{:S(2)}) collective-permute-start(f32[16,576]{1,0:T(8,128)S(1)} %fusion.1), channel_id=1, source_target_pairs={{0,7},{1,8},{2,9},{3,10},{4,11},{5,12},{6,13},{7,14},{8,15},{9,16}... | collective-permute-start | bytes 110600
  472.3 5.4 collective-permute-start.8
  475.4 3.3 collective-permute-start.9
Sparse Core Ops, SparseCore 0:
  74.2 47.5 reduce-scatter.7
  280.2 106.1 all-gather.5
  530.2 177.2 all-reduce.5
